TPU v7x, 128 devices: a whole 4x4x4 slice. The times are simulated.
128 devices in a mesh: row: 8 (over z_lo, x), col: 16 (over z_hi, y, core).
Axes of the slice: x: 4, y: 4, z: 4 (z_hi: 2, z_lo: 2; z = z_hi * 2 + z_lo), core: 2. Of those that a mesh axis runs over, the one named last changes fastest.
Arguments:
- trunk: bfloat16 [2048, 256], P(('row', 'col')), may hold values from -6 to 6
- row_weight: bfloat16 [256, 512], replicated, may hold values from -0.375 to 0.375
- column_weight: bfloat16 [256, 512], replicated, may hold values from -0.375 to 0.375
- pair_map_weight: bfloat16 [512, 48], replicated, may hold values from -0.25 to 0.25
- dilated_weight: bfloat16 [3, 3, 48, 48], replicated, may hold values from -0.3125 to 0.3125
- mixing_weight: bfloat16 [48, 48], replicated, may hold values from -0.875 to 0.875
Outputs:
- block_out: bfloat16 [48, 2048, 2048], P(None, 'row', 'col')
All inputs are finite; a program needn't handle non-finite values.
Results may differ from a plain program's by a relative error of at most 0.0067.
Values may be sent and summed in bfloat16 or wider, within the bound.
A program may use at most 128 MiB of HBM per device.

v0:
```python
import math

import jax
import jax.numpy as jnp
from jax import lax
from jax.sharding import PartitionSpec as P

DILATION_STEP = 8


def extended(cells, sides, width):
    for axis, dim in sides:
        count = lax.axis_size(axis)
        ends = count - 1
        head = lax.slice_in_dim(cells, 0, width, axis=dim)
        tail = lax.slice_in_dim(cells, cells.shape[dim] - width, cells.shape[dim], axis=dim)
        cells = jnp.concatenate(
            [
                lax.ppermute(tail, axis, [(i, (i + 1) % count) for i in range(ends)]),
                cells,
                lax.ppermute(head, axis, [((i + 1) % count, i) for i in range(ends)]),
            ],
            axis=dim,
        )
    return cells


def project(source, weight):
    return jnp.dot(source, weight, preferred_element_type=jnp.float32).astype(jnp.bfloat16)


def on_device(trunk, row_weight, column_weight, pair_map_weight, dilated_weight, mixing_weight):
    n_row = lax.axis_size("row")
    n_col = lax.axis_size("col")
    shard = trunk.shape[0]
    bins = shard * n_row * n_col
    row_device_index = bins // n_row
    column_device_index = bins // n_col
    width = row_weight.shape[1]
    row_idx = lax.axis_index("row")
    col_idx = lax.axis_index("col")
    moved = jnp.concatenate([project(trunk, row_weight), project(trunk, column_weight)], axis=1)
    gathered = lax.all_gather(moved, ("row", "col"), axis=0, tiled=True)
    row_src = lax.dynamic_slice_in_dim(gathered, row_idx * row_device_index, row_device_index, 0)
    col_src = lax.dynamic_slice_in_dim(
        gathered, col_idx * column_device_index, column_device_index, 0
    )
    row_proj = row_src[:, :width]
    col_proj = col_src[:, width:]
    blocksz = math.gcd(row_device_index, 64)
    count = row_device_index // blocksz

    def pair_rows(rows):
        pair_act = jnp.maximum(rows[:, None, :] + col_proj[None, :, :], jnp.zeros((), jnp.bfloat16))
        hidden = jnp.einsum(
            "ijk,ko->oij", pair_act, pair_map_weight, preferred_element_type=jnp.float32
        )
        return hidden.astype(jnp.bfloat16)

    stacked = lax.map(pair_rows, row_proj.reshape(count, blocksz, width))
    channels = pair_map_weight.shape[1]
    base = jnp.transpose(stacked, (1, 0, 2, 3)).reshape(
        channels, row_device_index, column_device_index
    )
    pair_activation = jnp.maximum(base, jnp.zeros((), jnp.bfloat16))
    padded_pairs = extended(pair_activation, (("row", 1), ("col", 2)), DILATION_STEP)
    total_sum = jnp.zeros((channels, row_device_index, column_device_index), jnp.float32)
    for first_tap_offset in range(3):
        for second_tap_offset in range(3):
            neighbour_window = padded_pairs[
                :,
                first_tap_offset * DILATION_STEP : first_tap_offset * DILATION_STEP
                + row_device_index,
                second_tap_offset * DILATION_STEP : second_tap_offset * DILATION_STEP
                + column_device_index,
            ]
            total_sum = total_sum + jnp.einsum(
                "zy,yea->zea",
                dilated_weight[first_tap_offset, second_tap_offset],
                neighbour_window,
                preferred_element_type=jnp.float32,
            )
    mid = jnp.maximum(total_sum, 0.0).astype(jnp.bfloat16)
    mixed = jnp.einsum("zy,yea->zea", mixing_weight, mid, preferred_element_type=jnp.float32)
    return (base.astype(jnp.float32) + mixed).astype(jnp.bfloat16)


def solution(mesh):
    return jax.shard_map(
        on_device,
        mesh=mesh,
        in_specs=(P(("row", "col"), None), P(), P(), P(), P(), P()),
        out_specs=P(None, "row", "col"),
        check_vma=False,
    )
```

profile of v0, /device:TPU:1, one launch (start us, length us, event | category | flops | bytes accessed | tf_op | source)
XLA Modules:
  0.0 338.2 jit_solution(14006106457405976920)
XLA Ops:
  10.1 201.0 %all-gather.2.cloned.1.call-done = bf16[2048,1024]{1,0:T(8,128)(2,1)} async-done(((bf16[16,1024]{1,0:T(8,128)(2,1)}), bf16[2048,1024]{1,0:T(8,128)(2,1)}) %all-gather.2.cloned.1.call-update) | async-done | bytes 4194320 | tf_op jit(solution)/shard_map/all_gather | solution.py:43
  213.0 14.4 %while.10 = (s32[]{:T(128)}, bf16[4,48,64,128]{3,1,2,0:T(8,128)(2,1)S(1)}, bf16[4,64,512]{2,1,0:T(8,128)(2,1)S(1)}, bf16[128,512]{1,0:T(8,128)(2,1)S(1)}, bf16[512,48]{0,1:T(8,128)(2,1)}, /*index=5*/s32[]{:T(128)}) while((s32[]{:T(128)}, bf16[4,48,64,128]{3,1,2,0:T(8,128)(2,1)S(1)}, bf16[4,64,512]{2,1,0:T(8,128)(2,1)S(1)}, ...), condition=%wide.region_1.2_spmd, body=%wide.region_0.1_spmd.sunk | while | flops 411435008 | bytes 1163341 | solution.py:60
  213.0 3.6 %fusion.87 = bf16[4,48,64,128]{3,1,2,0:T(8,128)(2,1)S(1)} fusion(bf16[4,48,64,128]{3,1,2,0:T(8,128)(2,1)S(1)} %get-tuple-element.90, s32[]{:T(128)} %get-tuple-element.89, bf16[128,512]{1,0:T(8,128)(2,1)S(1)} %get-tuple-element.98, bf16[64,512]{1,0:T(8,128)(2,1)S(1)} %dynamic-slice_bitcast_fusion.2, bf16[512,48]{0,1:T(8,128)(2,1)} %get-tuple-element.99), kind=kOutput, calls=%fused_computation.8.clone.1 | convolution fusion | flops 411435008 | bytes 1032196 | tf_op jit(solution)/shard_map/while/body/eval_jaxpr/ijk,ko->oij/dot_general | solution.py:55
  216.6 3.6 %fusion.87 = bf16[4,48,64,128]{3,1,2,0:T(8,128)(2,1)S(1)} fusion(bf16[4,48,64,128]{3,1,2,0:T(8,128)(2,1)S(1)} %get-tuple-element.90, s32[]{:T(128)} %get-tuple-element.89, bf16[128,512]{1,0:T(8,128)(2,1)S(1)} %get-tuple-element.98, bf16[64,512]{1,0:T(8,128)(2,1)S(1)} %dynamic-slice_bitcast_fusion.2, bf16[512,48]{0,1:T(8,128)(2,1)} %get-tuple-element.99), kind=kOutput, calls=%fused_computation.8.clone.1 | convolution fusion | flops 411435008 | bytes 1032196 | tf_op jit(solution)/shard_map/while/body/eval_jaxpr/ijk,ko->oij/dot_general | solution.py:55
  220.2 3.6 %fusion.87 = bf16[4,48,64,128]{3,1,2,0:T(8,128)(2,1)S(1)} fusion(bf16[4,48,64,128]{3,1,2,0:T(8,128)(2,1)S(1)} %get-tuple-element.90, s32[]{:T(128)} %get-tuple-element.89, bf16[128,512]{1,0:T(8,128)(2,1)S(1)} %get-tuple-element.98, bf16[64,512]{1,0:T(8,128)(2,1)S(1)} %dynamic-slice_bitcast_fusion.2, bf16[512,48]{0,1:T(8,128)(2,1)} %get-tuple-element.99), kind=kOutput, calls=%fused_computation.8.clone.1 | convolution fusion | flops 411435008 | bytes 1032196 | tf_op jit(solution)/shard_map/while/body/eval_jaxpr/ijk,ko->oij/dot_general | solution.py:55
  223.8 3.6 %fusion.87 = bf16[4,48,64,128]{3,1,2,0:T(8,128)(2,1)S(1)} fusion(bf16[4,48,64,128]{3,1,2,0:T(8,128)(2,1)S(1)} %get-tuple-element.90, s32[]{:T(128)} %get-tuple-element.89, bf16[128,512]{1,0:T(8,128)(2,1)S(1)} %get-tuple-element.98, bf16[64,512]{1,0:T(8,128)(2,1)S(1)} %dynamic-slice_bitcast_fusion.2, bf16[512,48]{0,1:T(8,128)(2,1)} %get-tuple-element.99), kind=kOutput, calls=%fused_computation.8.clone.1 | convolution fusion | flops 411435008 | bytes 1032196 | tf_op jit(solution)/shard_map/while/body/eval_jaxpr/ijk,ko->oij/dot_general | solution.py:55
  230.2 2.6 collective-permute-start
  238.2 4.3 %fusion.76 = (bf16[48,272,8]{2,0,1:T(8,128)(2,1)}, bf16[48,272,8]{2,0,1:T(8,128)(2,1)}) fusion(bf16[48,272,128]{2,0,1:T(8,128)(2,1)S(1)} %constant_dynamic-update-slice_fusion), kind=kLoop, calls=%fused_computation.83 | loop fusion | bytes 835584 | tf_op jit(solution)/shard_map/slice | solution.py:16
  242.5 5.0 %copy.18 = bf16[48,272,8]{1,2,0:T(8,128)(2,1)} copy(bf16[48,272,8]{2,0,1:T(8,128)(2,1)} %get-tuple-element.49) | data formatting | bytes 417792 | tf_op jit(solution)/shard_map/slice | solution.py:15
  247.5 4.4 %collective-permute-start.3 = (bf16[48,272,8]{1,2,0:T(8,128)(2,1)}, bf16[48,272,8]{1,2,0:T(8,128)(2,1)}, u32[]{:S(2)}, u32[]{:S(2)}) collective-permute-start(bf16[48,272,8]{1,2,0:T(8,128)(2,1)} %copy.18), channel_id=1, source_target_pairs={{1,0},{2,1},{3,2},{4,3},{5,4},{6,5},{7,6},{8,7},{9,8},{10,9},{11,1... | collective-permute-start | bytes 626696 | tf_op jit(solution)/shard_map/ppermute | solution.py:21
  251.9 5.0 %copy.15 = bf16[48,272,8]{1,2,0:T(8,128)(2,1)} copy(bf16[48,272,8]{2,0,1:T(8,128)(2,1)} %get-tuple-element.48) | data formatting | bytes 417792 | tf_op jit(solution)/shard_map/slice | solution.py:16
  257.0 3.0 collective-permute-start.2
  260.0 5.5 %fusion.32 = f32[256,128,48]{1,2,0:T(8,128)} fusion(bf16[48,8,128]{2,0,1:T(8,128)(2,1)S(1)} %collective-permute-done.1, bf16[48,256,128]{2,0,1:T(8,128)(2,1)} %copy-done.6, bf16[3,3,48,48]{3,2,1,0:T(8,128)(2,1)} %param.12), kind=kOutput, calls=%fused_computation.35 | convolution fusion | flops 157286400 | bytes 9547776 | tf_op jit(solution)/shard_map/zy,yea->zea/dot_general | solution.py:77
  265.5 4.3 %fusion.36 = f32[256,128,48]{1,2,0:T(8,128)} fusion(bf16[48,256,128]{2,0,1:T(8,128)(2,1)S(1)} %copy-done.7, bf16[48,8,128]{2,0,1:T(8,128)(2,1)S(1)} %collective-permute-done, bf16[3,3,48,48]{3,2,1,0:T(8,128)(2,1)} %param.12), kind=kOutput, calls=%fused_computation.41 | convolution fusion | flops 157286400 | bytes 9547776 | tf_op jit(solution)/shard_map/zy,yea->zea/dot_general | solution.py:77
  269.8 5.0 %copy.16 = bf16[48,272,8]{2,0,1:T(8,128)(2,1)} copy(bf16[48,272,8]{1,2,0:T(8,128)(2,1)} %collective-permute-done.2) | data formatting | bytes 417792 | tf_op jit(solution)/shard_map/ppermute | solution.py:19
  274.8 6.2 %fusion.25 = f32[256,128,48]{1,2,0:T(8,128)} fusion(bf16[48,272,8]{2,0,1:T(8,128)(2,1)} %copy.16, bf16[48,272,128]{2,0,1:T(8,128)(2,1)S(1)} %constant_dynamic-update-slice_fusion, bf16[3,3,48,48]{3,2,1,0:T(8,128)(2,1)S(1)} %copy-done.9), kind=kOutput, calls=%fused_computation.28 | convolution fusion | flops 157286400 | bytes 9854976 | tf_op jit(solution)/shard_map/zy,yea->zea/dot_general | solution.py:77
  281.1 3.5 %fusion.28 = f32[256,128,48]{1,2,0:T(8,128)} fusion(bf16[48,272,8]{2,0,1:T(8,128)(2,1)S(1)} %copy-done.2, bf16[48,272,128]{2,0,1:T(8,128)(2,1)S(1)} %constant_dynamic-update-slice_fusion, bf16[3,3,48,48]{3,2,1,0:T(8,128)(2,1)S(1)} %copy-done.9), kind=kOutput, calls=%fused_computation.30 | convolution fusion | flops 157286400 | bytes 12988416 | tf_op jit(solution)/shard_map/zy,yea->zea/dot_general | solution.py:77
  284.6 4.9 %copy.19 = bf16[48,272,8]{2,0,1:T(8,128)(2,1)} copy(bf16[48,272,8]{1,2,0:T(8,128)(2,1)} %collective-permute-done.3) | data formatting | bytes 417792 | tf_op jit(solution)/shard_map/ppermute | solution.py:21
  289.5 6.9 %fusion.22 = f32[256,128,48]{1,2,0:T(8,128)} fusion(bf16[48,272,128]{2,0,1:T(8,128)(2,1)S(1)} %constant_dynamic-update-slice_fusion, bf16[48,272,8]{2,0,1:T(8,128)(2,1)} %copy.19, bf16[3,3,48,48]{3,2,1,0:T(8,128)(2,1)S(1)} %copy-done.9), kind=kOutput, calls=%fused_computation.26 | convolution fusion | flops 157286400 | bytes 9854976 | tf_op jit(solution)/shard_map/zy,yea->zea/dot_general | solution.py:77
  296.4 4.1 %fusion.19 = f32[256,128,48]{1,2,0:T(8,128)} fusion(bf16[48,272,128]{2,0,1:T(8,128)(2,1)S(1)} %constant_dynamic-update-slice_fusion, bf16[48,272,8]{2,0,1:T(8,128)(2,1)S(1)} %copy-done.4, bf16[3,3,48,48]{3,2,1,0:T(8,128)(2,1)S(1)} %copy-done.9), kind=kOutput, calls=%fused_computation.24 | convolution fusion | flops 157286400 | bytes 12988416 | tf_op jit(solution)/shard_map/zy,yea->zea/dot_general | solution.py:77
  300.5 4.2 %fusion.34 = f32[256,128,48]{1,2,0:T(8,128)} fusion(bf16[48,272,128]{2,0,1:T(8,128)(2,1)S(1)} %constant_dynamic-update-slice_fusion, bf16[48,272,8]{2,0,1:T(8,128)(2,1)S(1)} %copy-done.3, bf16[3,3,48,48]{3,2,1,0:T(8,128)(2,1)S(1)} %copy-done.9), kind=kOutput, calls=%fused_computation.38 | convolution fusion | flops 157286400 | bytes 12988416 | tf_op jit(solution)/shard_map/zy,yea->zea/dot_general | solution.py:77
  304.8 4.8 %fusion.30 = f32[256,128,48]{1,2,0:T(8,128)} fusion(bf16[48,272,8]{2,0,1:T(8,128)(2,1)S(1)} %copy-done.4, bf16[48,272,128]{2,0,1:T(8,128)(2,1)S(1)} %constant_dynamic-update-slice_fusion, bf16[3,3,48,48]{3,2,1,0:T(8,128)(2,1)S(1)} %copy-done.9), kind=kOutput, calls=%fused_computation.32 | convolution fusion | flops 157286400 | bytes 12988416 | tf_op jit(solution)/shard_map/zy,yea->zea/dot_general | solution.py:77
  309.5 19.3 %fusion.17 = bf16[48,256,128]{2,0,1:T(8,128)(2,1)S(1)} fusion(f32[256,128,48]{1,2,0:T(8,128)} %fusion.30, f32[256,128,48]{1,2,0:T(8,128)} %fusion.32, f32[256,128,48]{1,2,0:T(8,128)} %fusion.34, f32[256,128,48]{1,2,0:T(8,128)} %fusion.19, f32[256,128,48]{1,2,0:T(8,128)} %fusion.25, f32[256,128,48]{1,2,0:T(8,128)} %fusion.22, f32[256,128,48]{1,2,0:T(8,128)} %fusion.28, ...), kind=kOutput, calls=%fused_computation.21 | convolution fusion | flops 322437120 | bytes 59793408 | tf_op jit(solution)/shard_map/zy,yea->zea/dot_general | solution.py:84
  328.9 2.5 copy.22
  (45 shorter events, 13.7 us)
Async XLA Ops:
  6.5 1.0 copy-start
  6.5 204.5 %all-gather.2.cloned.1.call-start = ((), (), s32[]{:S(2)}) async-start(), calls=%async_computation | async-start | bytes 4227072 | tf_op jit(solution)/shard_map/all_gather | solution.py:43
  227.3 2.9 copy-start.8
  228.2 8.6 %copy-start.5 = (bf16[4,48,64,128]{3,2,0,1:T(8,128)(2,1)}, bf16[4,48,64,128]{3,2,0,1:T(8,128)(2,1)S(1)}, u32[]{:S(2)}) copy-start(bf16[4,48,64,128]{3,2,0,1:T(8,128)(2,1)S(1)} %copy_maximum_fusion) | copy-start | bytes 9437188
  230.2 8.0 %copy-start.6 = (bf16[48,256,128]{2,0,1:T(8,128)(2,1)}, bf16[48,256,128]{2,0,1:T(8,128)(2,1)S(1)}, u32[]{:S(2)}) copy-start(bf16[48,256,128]{2,0,1:T(8,128)(2,1)S(1)} %copy.12) | copy-start | bytes 9437188
  230.2 4.2 %collective-permute-start = (bf16[48,8,128]{2,0,1:T(8,128)(2,1)S(1)}, bf16[48,8,128]{2,0,1:T(8,128)(2,1)S(1)}, u32[]{:S(2)}, u32[]{:S(2)}) collective-permute-start(bf16[48,8,128]{2,0,1:T(8,128)(2,1)S(1)} %get-tuple-element.51), channel_id=1, source_target_pairs={{0,16},{16,32},{32,48},{48,64},{64,80},{80,96},{96,112},{1,17},{17... | collective-permute-start | bytes 294920 | tf_op jit(solution)/shard_map/ppermute | solution.py:19
  232.9 5.4 %collective-permute-start.1 = (bf16[48,8,128]{2,0,1:T(8,128)(2,1)S(1)}, bf16[48,8,128]{2,0,1:T(8,128)(2,1)S(1)}, u32[]{:S(2)}, u32[]{:S(2)}) collective-permute-start(bf16[48,8,128]{2,0,1:T(8,128)(2,1)S(1)} %get-tuple-element.50), channel_id=1, source_target_pairs={{16,0},{32,16},{48,32},{64,48},{80,64},{96,80},{112,96},{17,1},{33... | collective-permute-start | bytes 294920 | tf_op jit(solution)/shard_map/ppermute | solution.py:21
  247.5 37.1 %collective-permute-start.3 = (bf16[48,272,8]{1,2,0:T(8,128)(2,1)}, bf16[48,272,8]{1,2,0:T(8,128)(2,1)}, u32[]{:S(2)}, u32[]{:S(2)}) collective-permute-start(bf16[48,272,8]{1,2,0:T(8,128)(2,1)} %copy.18), channel_id=1, source_target_pairs={{1,0},{2,1},{3,2},{4,3},{5,4},{6,5},{7,6},{8,7},{9,8},{10,9},{11,1... | collective-permute-start | bytes 626696 | tf_op jit(solution)/shard_map/ppermute | solution.py:21
  257.0 8.6 %copy-start.7 = (bf16[48,256,128]{2,0,1:T(8,128)(2,1)S(1)}, bf16[48,256,128]{2,0,1:T(8,128)(2,1)}, u32[]{:S(2)}) copy-start(bf16[48,256,128]{2,0,1:T(8,128)(2,1)} %copy-done.6) | copy-start | bytes 9437188
  257.0 12.8 %collective-permute-start.2 = (bf16[48,272,8]{1,2,0:T(8,128)(2,1)}, bf16[48,272,8]{1,2,0:T(8,128)(2,1)}, u32[]{:S(2)}, u32[]{:S(2)}) collective-permute-start(bf16[48,272,8]{1,2,0:T(8,128)(2,1)} %copy.15), channel_id=1, source_target_pairs={{0,1},{1,2},{2,3},{3,4},{4,5},{5,6},{6,7},{7,8},{8,9},{9,10},{10,1... | collective-permute-start | bytes 626696 | tf_op jit(solution)/shard_map/ppermute | solution.py:19
  269.8 5.0 %copy-start.9 = (bf16[3,3,48,48]{3,2,1,0:T(8,128)(2,1)S(1)}, bf16[3,3,48,48]{3,2,1,0:T(8,128)(2,1)}, u32[]{:S(2)}) copy-start(bf16[3,3,48,48]{3,2,1,0:T(8,128)(2,1)} %param.12) | copy-start | bytes 124420
  274.8 6.2 %copy-start.2 = (bf16[48,272,8]{2,0,1:T(8,128)(2,1)S(1)}, bf16[48,272,8]{2,0,1:T(8,128)(2,1)}, u32[]{:S(2)}) copy-start(bf16[48,272,8]{2,0,1:T(8,128)(2,1)} %copy.16) | copy-start | bytes 626692
  289.5 6.9 %copy-start.4 = (bf16[48,272,8]{2,0,1:T(8,128)(2,1)S(1)}, bf16[48,272,8]{2,0,1:T(8,128)(2,1)}, u32[]{:S(2)}) copy-start(bf16[48,272,8]{2,0,1:T(8,128)(2,1)} %copy.19) | copy-start | bytes 626692
  296.4 4.1 %copy-start.3 = (bf16[48,272,8]{2,0,1:T(8,128)(2,1)S(1)}, bf16[48,272,8]{2,0,1:T(8,128)(2,1)}, u32[]{:S(2)}) copy-start(bf16[48,272,8]{2,0,1:T(8,128)(2,1)} %copy.16) | copy-start | bytes 626692
  304.8 4.8 %copy-start.10 = (bf16[48,48]{1,0:T(8,128)(2,1)S(1)}, bf16[48,48]{1,0:T(8,128)(2,1)}, u32[]{:S(2)}) copy-start(bf16[48,48]{1,0:T(8,128)(2,1)} %param.13) | copy-start | bytes 13828
  309.5 21.8 %copy-start.1 = (bf16[256,512]{1,0:T(8,128)(2,1)S(1)}, bf16[256,512]{1,0:T(8,128)(2,1)}, u32[]{:S(2)}) copy-start(bf16[256,512]{1,0:T(8,128)(2,1)} %param.10) | copy-start | bytes 786436
Sparse Core Ops, SparseCore 0:
  10.2 200.8 all-gather.1
where the time goes:
time: 341 us; the launch traced here: 338 us
  waiting for transfers between devices  203 us (60%)
  matrix products  75.1 us (22%)
  local copies, waits for them, and re-layouts  33.9 us (10%)
  between operations  13.5 us (4%)
  starting transfers between devices  11.4 us (3%)
    all_gather x1, waiting for transfers between devices, on_device(): gathered = lax.all_gather(moved, ('row', 'col'), axis=0, tiled=True)  201 us
    dot_general x8, matrix products, on_device(): jnp.einsum('zy,yea->zea', dilated_weight[first_tap_offset, second_tap_off...  39.6 us
    dot_general x1, matrix products, on_device(): jnp.einsum('zy,yea->zea', mixing_weight, mid, preferred_element_type=jnp....  19.3 us
    dot_general x4, matrix products, pair_rows(): jnp.einsum('ijk,ko->oij', pair_act, pair_map_weight, preferred_element_ty...  14.2 us
    slice x2, local copies, waits for them, and re-layouts, extended(): lax.slice_in_dim(cells, cells.shape[dim] - width, cells.shape[dim], axis=...  9.27 us
  transfers between devices with their start and end apart: 5, of which 3 were waited for; matrix products, arithmetic and copies ran while one was open for 9% of the time, Pallas kernels for 0%

commit v1 on v0

v1 whole, which is shorter than its diff:
```python
import jax
import jax.numpy as jnp
from jax import lax
from jax.experimental import pallas as pl
from jax.experimental.pallas import tpu as pltpu
from jax.sharding import PartitionSpec as P

bf16 = jnp.bfloat16
f32 = jnp.float32
MESH = pl.DeviceIdType.MESH
VMEM = pl.BlockSpec(memory_space=pltpu.VMEM)


def gather_kernel(x_ref, rows_ref, cols_ref, zero_ref, send_sem, rows_sem, cols_sem):
    r = lax.axis_index("row")
    c = lax.axis_index("col")
    k = lax.rem(c, 8)
    home = 2 * r + c // 8
    barrier = pltpu.get_barrier_semaphore()
    zero_ref[...] = jnp.zeros_like(zero_ref)

    def signal(row, col):
        pl.semaphore_signal(barrier, inc=1, device_id=(row, col), device_id_type=MESH)

    def each(count, body):
        def step(n, carry):
            body(n)
            return carry

        lax.fori_loop(0, count, step, 0)

    each(15, lambda n: signal(r, lax.rem(c + 1 + n, 16)))

    @pl.when(r > 0)
    def _():
        signal(r - 1, 15)

    @pl.when(r < 7)
    def _():
        signal(r + 1, 0)

    def signal_column_source(n):
        row, col = c // 2, 8 * lax.rem(c, 2) + n

        @pl.when((row != r) | (col != c))
        def _():
            signal(row, col)

    each(8, signal_column_source)

    @pl.when(c > 0)
    def _():
        row, col = (c - 1) // 2, 8 * lax.rem(c - 1, 2) + 7

        @pl.when((row != r) | (col != c))
        def _():
            signal(row, col)

    @pl.when(c < 15)
    def _():
        row, col = (c + 1) // 2, 8 * lax.rem(c + 1, 2)

        @pl.when((row != r) | (col != c))
        def _():
            signal(row, col)

    low_halo_rows = (c == 15) & (r < 7)
    high_halo_rows = (c == 0) & (r > 0)
    low_halo_cols = (k == 7) & (home < 15)
    high_halo_cols = (k == 0) & (home > 0)

    def away(col):
        return 7 + (col != c).astype(jnp.int32)

    peers = 15 + away(home)
    peers += 16 * (low_halo_rows | high_halo_rows).astype(jnp.int32)
    peers += low_halo_cols.astype(jnp.int32) * away(home + 1)
    peers += high_halo_cols.astype(jnp.int32) * away(home - 1)
    pl.semaphore_wait(barrier, peers)

    def remote(src, dst, sem, row, col):
        return pltpu.make_async_remote_copy(
            src_ref=src, dst_ref=dst, send_sem=send_sem, recv_sem=sem, device_id=(row, col), device_id_type=MESH
        )

    own_rows = rows_ref.at[pl.ds(1 + 2 * c, 2)]
    own_cols = cols_ref.at[pl.ds(1 + 2 * k, 2)]

    def to_column(src, dst, col):
        def body(n):
            row = lax.rem(r + n, 8)
            other = (row != r) | (col != c)

            @pl.when(other)
            def _():
                remote(src, dst, cols_sem, row, col).start()

            @pl.when(jnp.logical_not(other))
            def _():
                pltpu.make_async_copy(src, dst, cols_sem).start()

        each(8, body)

    @pl.when(low_halo_rows)
    def _():
        each(16, lambda n: remote(x_ref.at[1], rows_ref.at[0], rows_sem, r + 1, n).start())

    @pl.when(high_halo_rows)
    def _():
        each(16, lambda n: remote(x_ref.at[0], rows_ref.at[33], rows_sem, r - 1, n).start())

    @pl.when(low_halo_cols)
    def _():
        to_column(x_ref.at[1], cols_ref.at[0], home + 1)

    @pl.when(high_halo_cols)
    def _():
        to_column(x_ref.at[0], cols_ref.at[17], home - 1)

    to_column(x_ref, own_cols, home)
    each(15, lambda n: remote(x_ref, own_rows, rows_sem, r, lax.rem(c + 1 + n, 16)).start())
    pltpu.make_async_copy(x_ref, own_rows, rows_sem).start()

    @pl.when(r == 0)
    def _():
        pltpu.make_async_copy(zero_ref, rows_ref.at[0], rows_sem).start()

    @pl.when(r == 7)
    def _():
        pltpu.make_async_copy(zero_ref, rows_ref.at[33], rows_sem).start()

    @pl.when(c == 0)
    def _():
        pltpu.make_async_copy(zero_ref, cols_ref.at[0], cols_sem).start()

    @pl.when(c == 15)
    def _():
        pltpu.make_async_copy(zero_ref, cols_ref.at[17], cols_sem).start()

    def sent(blocks):
        part = rows_ref.at[pl.ds(0, blocks)]
        pltpu.make_async_copy(part, part, send_sem).wait()

    sent(30)

    sent(14)

    @pl.when(home != c)
    def _():
        sent(2)

    @pl.when(low_halo_rows)
    def _():
        sent(16)

    @pl.when(high_halo_rows)
    def _():
        sent(16)

    def column_sent(col):
        sent(7)

        @pl.when(col != c)
        def _():
            sent(1)

    @pl.when(low_halo_cols)
    def _():
        column_sent(home + 1)

    @pl.when(high_halo_cols)
    def _():
        column_sent(home - 1)

    pltpu.make_async_copy(rows_ref, rows_ref, rows_sem).wait()
    pltpu.make_async_copy(cols_ref, cols_ref, cols_sem).wait()


def gather(trunk):
    width = trunk.shape[1]
    return pl.pallas_call(
        gather_kernel,
        out_shape=(
            jax.ShapeDtypeStruct((34, 8, width), bf16),
            jax.ShapeDtypeStruct((18, 8, width), bf16),
        ),
        in_specs=[VMEM],
        out_specs=(VMEM, VMEM),
        scratch_shapes=[
            pltpu.VMEM((8, width), bf16),
            pltpu.SemaphoreType.DMA,
            pltpu.SemaphoreType.DMA,
            pltpu.SemaphoreType.DMA,
        ],
        compiler_params=pltpu.CompilerParams(collective_id=0, has_side_effects=True),
        name="gather_bins",
    )(trunk.reshape(2, 8, width))


def dot(a, b, dims=((1,), (0,))):
    return lax.dot_general(a, b, (dims, ((), ())), preferred_element_type=f32)


def block_kernel(
    rows_ref, cols_ref, row_w_ref, col_w_ref, pair_w_ref, taps_ref, mix_ref, out_ref, row_pat, col_pat, act, base, taps, turn
):
    r = lax.axis_index("row")
    c = lax.axis_index("col")
    row_w = row_w_ref[...].T
    col_w = col_w_ref[...].T
    pair_w = pair_w_ref[...].T
    for a in range(3):
        for b in range(3):
            taps[48 * b : 48 * b + 48, 48 * a : 48 * a + 48] = taps_ref[a, b]
    for n in range(9):
        row_cells = []
        col_cells = []
        for p in (2 * n, 2 * n + 1):
            for e in range(2):
                bins = rows_ref[16 * e + p].astype(f32)
                row_cells.append(jnp.broadcast_to(bins[:, None, :], (8, 8, 256)).reshape(64, 256))
            bins = cols_ref[p].astype(f32)
            col_cells.append(jnp.broadcast_to(bins[None], (16, 8, 256)).reshape(128, 256))
        proj = dot(row_w, jnp.concatenate(row_cells, 0).astype(bf16), ((1,), (1,))).astype(bf16)
        row_pat[2 * n] = proj[:, :128]
        row_pat[2 * n + 1] = proj[:, 128:]
        proj = dot(col_w, jnp.concatenate(col_cells, 0).astype(bf16), ((1,), (1,))).astype(bf16)
        col_pat[2 * n] = proj[:, :128]
        col_pat[2 * n + 1] = proj[:, 128:]

    lane = lax.broadcasted_iota(jnp.int32, (1, 128), 1)
    zero = jnp.zeros((), bf16)

    def pair_rows(p, carry):
        row = row_pat[p]
        tile_row = 32 * r + 16 * (lane // 64) + p - 1
        inside = ((tile_row >= 0) & (tile_row < 256)).astype(f32)
        first = inside * (c > 0).astype(f32)
        last = inside * (c < 15).astype(f32)
        at = pl.ds(pl.multiple_of(48 * p, 16), 48)
        for n in range(9):
            pair_act = jnp.concatenate(
                [jnp.maximum(row + col_pat[2 * n], zero), jnp.maximum(row + col_pat[2 * n + 1], zero)], axis=1
            )
            hidden = dot(pair_w, pair_act)
            keep = jnp.concatenate([first if n == 0 else inside, last if n == 8 else inside], axis=1)
            act[at, 256 * n : 256 * n + 256] = (jnp.maximum(hidden, 0.0) * keep).astype(bf16)
            base[at, 256 * n : 256 * n + 256] = hidden.astype(bf16)
        return carry

    lax.fori_loop(0, 18, pair_rows, 0)

    mix = mix_ref[...]
    tap_w = taps[...]
    group = lane // 8

    def conv_rows(m, carry):
        for u in range(2):
            p = 2 * m + u
            at = pl.ds(pl.multiple_of(48 * p, 16), 144)
            parts = [dot(tap_w, act[at, 256 * n : 256 * n + 256]) for n in range(9)]

            def part(b, q):
                return parts[q // 2][48 * b : 48 * b + 48, 128 * (q % 2) : 128 * (q % 2) + 128]

            tiles = []
            for n in range(8):
                mids = [
                    jnp.maximum(part(0, q - 1) + part(1, q) + part(2, q + 1), 0.0).astype(bf16)
                    for q in (2 * n + 1, 2 * n + 2)
                ]
                here = base[pl.ds(pl.multiple_of(48 * (p + 1), 16), 48), 256 * n + 128 : 256 * n + 384]
                cells = (dot(mix, jnp.concatenate(mids, axis=1)) + here.astype(f32)).astype(bf16)
                tiles += [cells[:, :128], cells[:, 128:]]
            for d in (1, 2, 4, 8):
                stay = (group & d) == 0
                for q in range(16):
                    if q & d == 0:
                        x, y = tiles[q], tiles[q + d]
                        tiles[q] = jnp.where(stay, x, pltpu.roll(y, 8 * d, 1))
                        tiles[q + d] = jnp.where(stay, pltpu.roll(x, 128 - 8 * d, 1), y)
            for k in range(16):
                turn[k // 8, pl.ds(8 * u + k % 8, 48, stride=16), :] = tiles[k].astype(f32)
        for e in range(2):
            out_ref[:, pl.ds(pl.multiple_of(128 * e + 16 * m, 16), 16), :] = turn[e].reshape(48, 16, 128).astype(bf16)
        return carry

    lax.fori_loop(0, 8, conv_rows, 0)


def on_device(trunk, row_weight, column_weight, pair_map_weight, dilated_weight, mixing_weight):
    rows, cols = gather(trunk)
    return pl.pallas_call(
        block_kernel,
        out_shape=jax.ShapeDtypeStruct((48, 256, 128), bf16),
        in_specs=[VMEM] * 7,
        out_specs=VMEM,
        scratch_shapes=[
            pltpu.VMEM((18, 512, 128), bf16),
            pltpu.VMEM((18, 512, 128), bf16),
            pltpu.VMEM((18 * 48, 18 * 128), bf16),
            pltpu.VMEM((18 * 48, 18 * 128), bf16),
            pltpu.VMEM((144, 144), bf16),
            pltpu.VMEM((2, 768, 128), f32),
        ],
        compiler_params=pltpu.CompilerParams(vmem_limit_bytes=48 << 20),
        name="pair_block",
    )(rows, cols, row_weight, column_weight, pair_map_weight, dilated_weight, mixing_weight)


def solution(mesh):
    return jax.shard_map(
        on_device,
        mesh=mesh,
        in_specs=(P(("row", "col"), None), P(), P(), P(), P(), P()),
        out_specs=P(None, "row", "col"),
        check_vma=False,
    )
```

time: 341 us -> 45.1 us (0.13)
  waiting for transfers between devices: 203 us -> 0 us
  matrix products: 75.1 us -> 0 us
  Pallas kernels: 0 us -> 38.5 us
  local copies, waits for them, and re-layouts: 33.9 us -> 6.2 us
  between operations: 13.5 us -> 0.03 us
  starting transfers between devices: 11.4 us -> 0 us
    all_gather x1 -> x0, waiting for transfers between devices: 201 us -> none  [on_device(): gathered = lax.all_gather(moved, ('row', 'col'), axis=0, tiled=True)]
    dot_general x15 -> x0, matrix products: 75.1 us -> none  [the longest x8 39.6 us: on_device(): jnp.einsum('zy,yea->zea', dilated_weight[first_tap_offset, second_tap_off...]
    pallas_call x0 -> x2, Pallas kernels: none -> 38.5 us  [the longest x1 24.6 us: on_device(): pl.pallas_call(block_kernel, out_shape=jax.ShapeDtypeStruct((48, 256, 128...]
    slice x6 -> x0, local copies, waits for them, and re-layouts: 16.2 us -> none  [the longest x2 9.27 us: extended(): lax.slice_in_dim(cells, cells.shape[dim] - width, cells.shape[dim], axis=...]
    ppermute x4 -> x0, starting transfers between devices: 11.3 us -> none  [the longest x2 5.74 us: extended(): lax.ppermute(head, axis, [((i + 1) % count, i) for i in range(ends)])]
    ppermute x2 -> x0, local copies, waits for them, and re-layouts: 9.97 us -> none  [the longest x1 5.03 us: extended(): lax.ppermute(tail, axis, [(i, (i + 1) % count) for i in range(ends)])]
  transfers between devices with their start and end apart: 5 -> 0, of which waited for: 3 -> 0; matrix products, arithmetic and copies ran while one was open for 9% -> 0% of each run, Pallas kernels for 0% -> 0%
where the time goes in v1:
time: 45.1 us; the launch traced here: 44.7 us
  Pallas kernels  38.5 us (85%)
  local copies, waits for them, and re-layouts  6.2 us (14%)
    pallas_call x1, Pallas kernels, on_device(): pl.pallas_call(block_kernel, out_shape=jax.ShapeDtypeStruct((48, 256, 128...  24.6 us
    pallas_call x1, Pallas kernels, gather(): pl.pallas_call(gather_kernel, out_shape=(jax.ShapeDtypeStruct((34, 8, wid...  13.9 us
    unnamed x13, local copies, waits for them, and re-layouts  6.2 us

profile of v1, /device:TPU:1, one launch (start us, length us, event | category | flops | bytes accessed | tf_op | source)
XLA Modules:
  0.0 44.7 jit_solution(10401232665922003095)
XLA Ops:
  0.0 0.9 %copy.7.pair_w_ref = bf16[512,48]{1,0:T(8,128)(2,1)S(1)} copy(bf16[512,48]{0,1:T(8,128)(2,1)} %param.9) | data formatting | bytes 98304 | tf_op args[3]
  0.9 13.9 %gather_bins.1 = (bf16[34,8,256]{2,1,0:T(8,128)(2,1)}, bf16[18,8,256]{2,1,0:T(8,128)(2,1)}) custom-call(bf16[2,8,256]{2,1,0:T(8,128)(2,1)} %bitcast.1), custom_call_target="tpu_custom_call" | custom-call | tf_op jit(solution)/shard_map/gather_bins/pallas_call | solution.py:181
  14.8 0.0 copy-start
  14.8 0.9 %copy-done = bf16[256,512]{1,0:T(8,128)(2,1)S(1)} copy-done((bf16[256,512]{1,0:T(8,128)(2,1)S(1)}, bf16[256,512]{1,0:T(8,128)(2,1)}, u32[]{:S(2)}) %copy-start) | copy-done | bytes 262168
  15.8 0.0 copy-start.1
  15.8 0.9 %copy-done.1 = bf16[256,512]{1,0:T(8,128)(2,1)S(1)} copy-done((bf16[256,512]{1,0:T(8,128)(2,1)S(1)}, bf16[256,512]{1,0:T(8,128)(2,1)}, u32[]{:S(2)}) %copy-start.1) | copy-done | bytes 262168
  16.7 0.0 copy-start.2
  16.7 0.9 %copy-done.2 = bf16[34,8,256]{2,1,0:T(8,128)(2,1)S(1)} copy-done((bf16[34,8,256]{2,1,0:T(8,128)(2,1)S(1)}, bf16[34,8,256]{2,1,0:T(8,128)(2,1)}, u32[]{:S(2)}) %copy-start.2) | copy-done | bytes 139288
  17.6 0.0 copy-start.3
  17.6 0.9 %copy-done.3 = bf16[3,3,48,48]{3,2,1,0:T(8,128)(2,1)S(1)} copy-done((bf16[3,3,48,48]{3,2,1,0:T(8,128)(2,1)S(1)}, bf16[3,3,48,48]{3,2,1,0:T(8,128)(2,1)}, u32[]{:S(2)}) %copy-start.3) | copy-done | bytes 41496
  18.5 0.0 copy-start.4
  18.5 0.9 %copy-done.4 = bf16[18,8,256]{2,1,0:T(8,128)(2,1)S(1)} copy-done((bf16[18,8,256]{2,1,0:T(8,128)(2,1)S(1)}, bf16[18,8,256]{2,1,0:T(8,128)(2,1)}, u32[]{:S(2)}) %copy-start.4) | copy-done | bytes 73752
  19.4 0.0 copy-start.5
  19.4 0.7 %copy-done.5 = bf16[48,48]{1,0:T(8,128)(2,1)S(1)} copy-done((bf16[48,48]{1,0:T(8,128)(2,1)S(1)}, bf16[48,48]{1,0:T(8,128)(2,1)}, u32[]{:S(2)}) %copy-start.5) | copy-done | bytes 4632
  20.1 24.6 %pair_block.1 = bf16[48,256,128]{2,1,0:T(8,128)(2,1)} custom-call(bf16[34,8,256]{2,1,0:T(8,128)(2,1)S(1)} %copy-done.2, bf16[18,8,256]{2,1,0:T(8,128)(2,1)S(1)} %copy-done.4, bf16[256,512]{1,0:T(8,128)(2,1)S(1)} %copy-done, bf16[256,512]{1,0:T(8,128)(2,1)S(1)} %copy-done.1, bf16[512,48]{1,0:T(8,128)(2,1)S(1)} %copy.7.pair_w_ref, ...), custom_call_target="tpu_custom_call" | custom-call | tf_op jit(solution)/shard_map/pair_block/pallas_call | solution.py:293
Async XLA Ops:
  14.8 1.0 %copy-start = (bf16[256,512]{1,0:T(8,128)(2,1)S(1)}, bf16[256,512]{1,0:T(8,128)(2,1)}, u32[]{:S(2)}) copy-start(bf16[256,512]{1,0:T(8,128)(2,1)} %row_w_ref.1) | copy-start | bytes 786436
  15.8 0.9 %copy-start.1 = (bf16[256,512]{1,0:T(8,128)(2,1)S(1)}, bf16[256,512]{1,0:T(8,128)(2,1)}, u32[]{:S(2)}) copy-start(bf16[256,512]{1,0:T(8,128)(2,1)} %col_w_ref.1) | copy-start | bytes 786436
  16.7 0.9 %copy-start.2 = (bf16[34,8,256]{2,1,0:T(8,128)(2,1)S(1)}, bf16[34,8,256]{2,1,0:T(8,128)(2,1)}, u32[]{:S(2)}) copy-start(bf16[34,8,256]{2,1,0:T(8,128)(2,1)} %get-tuple-element.7.rows_ref) | copy-start | bytes 417796
  17.6 0.9 %copy-start.3 = (bf16[3,3,48,48]{3,2,1,0:T(8,128)(2,1)S(1)}, bf16[3,3,48,48]{3,2,1,0:T(8,128)(2,1)}, u32[]{:S(2)}) copy-start(bf16[3,3,48,48]{3,2,1,0:T(8,128)(2,1)} %taps_ref.1) | copy-start | bytes 124420
  18.5 0.9 %copy-start.4 = (bf16[18,8,256]{2,1,0:T(8,128)(2,1)S(1)}, bf16[18,8,256]{2,1,0:T(8,128)(2,1)}, u32[]{:S(2)}) copy-start(bf16[18,8,256]{2,1,0:T(8,128)(2,1)} %get-tuple-element.8.cols_ref) | copy-start | bytes 221188
  19.4 0.7 %copy-start.5 = (bf16[48,48]{1,0:T(8,128)(2,1)S(1)}, bf16[48,48]{1,0:T(8,128)(2,1)}, u32[]{:S(2)}) copy-start(bf16[48,48]{1,0:T(8,128)(2,1)} %mix_ref.1) | copy-start | bytes 13828

commit v2 on v1

--- a/solution.py
+++ b/solution.py
@@ -202,34 +202,59 @@
 
 
 def block_kernel(
-    rows_ref, cols_ref, row_w_ref, col_w_ref, pair_w_ref, taps_ref, mix_ref, out_ref, row_pat, col_pat, act, base, taps, turn
+    rows_hbm, cols_hbm, row_w_hbm, col_w_hbm, pair_w_hbm, taps_hbm, mix_hbm, out_hbm,
+    rows_in, cols_in, row_w_in, col_w_in, pair_w_in, taps_in, mix_in,
+    row_pat, col_pat, act, base, taps, turn, out_tile, in_sem, out_sem,
 ):
     r = lax.axis_index("row")
     c = lax.axis_index("col")
-    row_w = row_w_ref[...].T
-    col_w = col_w_ref[...].T
-    pair_w = pair_w_ref[...].T
+    loads = [
+        pltpu.make_async_copy(src, dst, in_sem.at[n])
+        for n, (src, dst) in enumerate(
+            (
+                (row_w_hbm, row_w_in),
+                (rows_hbm, rows_in),
+                (col_w_hbm, col_w_in),
+                (cols_hbm, cols_in),
+                (taps_hbm, taps_in),
+                (pair_w_hbm, pair_w_in),
+                (mix_hbm, mix_in),
+            )
+        )
+    ]
+    for load in loads:
+        load.start()
+
+    loads[0].wait()
+    row_w = row_w_in[...].T
+    loads[1].wait()
+    for n in range(9):
+        cells = []
+        for p in (2 * n, 2 * n + 1):
+            for e in range(2):
+                bins = rows_in[16 * e + p].astype(f32)
+                cells.append(jnp.broadcast_to(bins[:, None, :], (8, 8, 256)).reshape(64, 256))
+        proj = dot(row_w, jnp.concatenate(cells, 0).astype(bf16), ((1,), (1,))).astype(bf16)
+        row_pat[2 * n] = proj[:, :128]
+        row_pat[2 * n + 1] = proj[:, 128:]
+    loads[2].wait()
+    col_w = col_w_in[...].T
+    loads[3].wait()
+    for n in range(9):
+        cells = [jnp.broadcast_to(cols_in[q].astype(f32)[None], (16, 8, 256)).reshape(128, 256) for q in (2 * n, 2 * n + 1)]
+        proj = dot(col_w, jnp.concatenate(cells, 0).astype(bf16), ((1,), (1,))).astype(bf16)
+        col_pat[2 * n] = proj[:, :128]
+        col_pat[2 * n + 1] = proj[:, 128:]
+    loads[4].wait()
     for a in range(3):
         for b in range(3):
-            taps[48 * b : 48 * b + 48, 48 * a : 48 * a + 48] = taps_ref[a, b]
-    for n in range(9):
-        row_cells = []
-        col_cells = []
-        for p in (2 * n, 2 * n + 1):
-            for e in range(2):
-                bins = rows_ref[16 * e + p].astype(f32)
-                row_cells.append(jnp.broadcast_to(bins[:, None, :], (8, 8, 256)).reshape(64, 256))
-            bins = cols_ref[p].astype(f32)
-            col_cells.append(jnp.broadcast_to(bins[None], (16, 8, 256)).reshape(128, 256))
-        proj = dot(row_w, jnp.concatenate(row_cells, 0).astype(bf16), ((1,), (1,))).astype(bf16)
-        row_pat[2 * n] = proj[:, :128]
-        row_pat[2 * n + 1] = proj[:, 128:]
-        proj = dot(col_w, jnp.concatenate(col_cells, 0).astype(bf16), ((1,), (1,))).astype(bf16)
-        col_pat[2 * n] = proj[:, :128]
-        col_pat[2 * n + 1] = proj[:, 128:]
+            taps[48 * b : 48 * b + 48, 48 * a : 48 * a + 48] = taps_in[a, b]
+    loads[5].wait()
+    loads[6].wait()
 
     lane = lax.broadcasted_iota(jnp.int32, (1, 128), 1)
     zero = jnp.zeros((), bf16)
+    pair_w = pair_w_in[...]
 
     def pair_rows(p, carry):
         row = row_pat[p]
@@ -250,11 +275,17 @@
 
     lax.fori_loop(0, 18, pair_rows, 0)
 
-    mix = mix_ref[...]
+    mix = mix_in[...]
     tap_w = taps[...]
     group = lane // 8
 
+    def store(slot, e, m):
+        return pltpu.make_async_copy(
+            out_tile.at[slot, e], out_hbm.at[:, pl.ds(pl.multiple_of(128 * e + 16 * m, 16), 16), :], out_sem.at[slot, e]
+        )
+
     def conv_rows(m, carry):
+        slot = lax.rem(m, 2)
         for u in range(2):
             p = 2 * m + u
             at = pl.ds(pl.multiple_of(48 * p, 16), 144)
@@ -281,31 +312,56 @@
                         tiles[q + d] = jnp.where(stay, pltpu.roll(x, 128 - 8 * d, 1), y)
             for k in range(16):
                 turn[k // 8, pl.ds(8 * u + k % 8, 48, stride=16), :] = tiles[k].astype(f32)
+
+        @pl.when(m >= 2)
+        def _():
+            for e in range(2):
+                store(slot, e, m - 2).wait()
+
         for e in range(2):
-            out_ref[:, pl.ds(pl.multiple_of(128 * e + 16 * m, 16), 16), :] = turn[e].reshape(48, 16, 128).astype(bf16)
+            out_tile[slot, e] = turn[e].reshape(48, 16, 128).astype(bf16)
+            store(slot, e, m).start()
         return carry
 
     lax.fori_loop(0, 8, conv_rows, 0)
-
-
-def on_device(trunk, row_weight, column_weight, pair_map_weight, dilated_weight, mixing_weight):
-    rows, cols = gather(trunk)
+    for m in (6, 7):
+        for e in range(2):
+            store(m % 2, e, m).wait()
+
+
+def block(rows, cols, row_weight, column_weight, pair_map_weight, dilated_weight, mixing_weight):
+    hbm = pl.BlockSpec(memory_space=pltpu.HBM)
     return pl.pallas_call(
         block_kernel,
         out_shape=jax.ShapeDtypeStruct((48, 256, 128), bf16),
-        in_specs=[VMEM] * 7,
-        out_specs=VMEM,
+        in_specs=[hbm] * 7,
+        out_specs=hbm,
         scratch_shapes=[
+            pltpu.VMEM((34, 8, 256), bf16),
+            pltpu.VMEM((18, 8, 256), bf16),
+            pltpu.VMEM((256, 512), bf16),
+            pltpu.VMEM((256, 512), bf16),
+            pltpu.VMEM((48, 512), bf16),
+            pltpu.VMEM((3, 3, 48, 48), bf16),
+            pltpu.VMEM((48, 48), bf16),
             pltpu.VMEM((18, 512, 128), bf16),
             pltpu.VMEM((18, 512, 128), bf16),
             pltpu.VMEM((18 * 48, 18 * 128), bf16),
             pltpu.VMEM((18 * 48, 18 * 128), bf16),
             pltpu.VMEM((144, 144), bf16),
             pltpu.VMEM((2, 768, 128), f32),
+            pltpu.VMEM((2, 2, 48, 16, 128), bf16),
+            pltpu.SemaphoreType.DMA((7,)),
+            pltpu.SemaphoreType.DMA((2, 2)),
         ],
         compiler_params=pltpu.CompilerParams(vmem_limit_bytes=48 << 20),
         name="pair_block",
-    )(rows, cols, row_weight, column_weight, pair_map_weight, dilated_weight, mixing_weight)
+    )(rows, cols, row_weight, column_weight, pair_map_weight.T, dilated_weight, mixing_weight)
+
+
+def on_device(trunk, row_weight, column_weight, pair_map_weight, dilated_weight, mixing_weight):
+    rows, cols = gather(trunk)
+    return block(rows, cols, row_weight, column_weight, pair_map_weight, dilated_weight, mixing_weight)
 
 
 def solution(mesh):

time: 45.1 us -> 46.5 us (1.031)
  Pallas kernels: 38.5 us -> 40 us
    pallas_call x1, Pallas kernels: 24.6 us -> 26.2 us  [block(): pl.pallas_call(block_kernel, out_shape=jax.ShapeDtypeStruct((48, 256, 128...]
    unnamed x13 -> x14, local copies, waits for them, and re-layouts: 6.2 us -> 6.09 us
where the time goes in v2:
time: 46.5 us; the launch traced here: 46.1 us
  Pallas kernels  40 us (86%)
  local copies, waits for them, and re-layouts  6.09 us (13%)
    pallas_call x1, Pallas kernels, block(): pl.pallas_call(block_kernel, out_shape=jax.ShapeDtypeStruct((48, 256, 128...  26.2 us
    pallas_call x1, Pallas kernels, gather(): pl.pallas_call(gather_kernel, out_shape=(jax.ShapeDtypeStruct((34, 8, wid...  13.9 us
    unnamed x14, local copies, waits for them, and re-layouts  6.09 us

profile of v2, /device:TPU:1, one launch (start us, length us, event | category | flops | bytes accessed | tf_op | source)
XLA Modules:
  0.0 46.1 jit_solution(9265147813903834043)
XLA Ops:
  0.0 13.9 %gather_bins.1 = (bf16[34,8,256]{2,1,0:T(8,128)(2,1)}, bf16[18,8,256]{2,1,0:T(8,128)(2,1)}) custom-call(bf16[2,8,256]{2,1,0:T(8,128)(2,1)} %bitcast.3), custom_call_target="tpu_custom_call" | custom-call | tf_op jit(solution)/shard_map/gather_bins/pallas_call | solution.py:181
  13.9 0.0 copy-start
  13.9 0.9 %copy-done = bf16[256,512]{1,0:T(8,128)(2,1)S(1)} copy-done((bf16[256,512]{1,0:T(8,128)(2,1)S(1)}, bf16[256,512]{1,0:T(8,128)(2,1)}, u32[]{:S(2)}) %copy-start) | copy-done | bytes 262168
  14.8 0.0 copy-start.1
  14.8 0.9 %copy-done.1 = bf16[256,512]{1,0:T(8,128)(2,1)S(1)} copy-done((bf16[256,512]{1,0:T(8,128)(2,1)S(1)}, bf16[256,512]{1,0:T(8,128)(2,1)}, u32[]{:S(2)}) %copy-start.1) | copy-done | bytes 262168
  15.8 0.0 copy-start.2
  15.8 0.9 %copy-done.2 = bf16[34,8,256]{2,1,0:T(8,128)(2,1)S(1)} copy-done((bf16[34,8,256]{2,1,0:T(8,128)(2,1)S(1)}, bf16[34,8,256]{2,1,0:T(8,128)(2,1)}, u32[]{:S(2)}) %copy-start.2) | copy-done | bytes 139288
  16.7 0.0 copy-start.3
  16.7 0.9 %copy-done.3 = bf16[3,3,48,48]{3,2,1,0:T(8,128)(2,1)S(1)} copy-done((bf16[3,3,48,48]{3,2,1,0:T(8,128)(2,1)S(1)}, bf16[3,3,48,48]{3,2,1,0:T(8,128)(2,1)}, u32[]{:S(2)}) %copy-start.3) | copy-done | bytes 41496
  17.6 0.0 copy-start.4
  17.6 0.9 %copy-done.4 = bf16[18,8,256]{2,1,0:T(8,128)(2,1)S(1)} copy-done((bf16[18,8,256]{2,1,0:T(8,128)(2,1)S(1)}, bf16[18,8,256]{2,1,0:T(8,128)(2,1)}, u32[]{:S(2)}) %copy-start.4) | copy-done | bytes 73752
  18.5 0.0 copy-start.5
  18.5 0.8 %copy-done.5 = bf16[512,48]{0,1:T(8,128)(2,1)S(1)} copy-done((bf16[512,48]{0,1:T(8,128)(2,1)S(1)}, bf16[512,48]{0,1:T(8,128)(2,1)}, u32[]{:S(2)}) %copy-start.5) | copy-done | bytes 49176
  19.3 0.0 copy-start.6
  19.3 0.7 %copy-done.6 = bf16[48,48]{1,0:T(8,128)(2,1)S(1)} copy-done((bf16[48,48]{1,0:T(8,128)(2,1)S(1)}, bf16[48,48]{1,0:T(8,128)(2,1)}, u32[]{:S(2)}) %copy-start.6) | copy-done | bytes 4632
  20.0 26.2 %pair_block.1 = bf16[48,256,128]{2,1,0:T(8,128)(2,1)} custom-call(bf16[34,8,256]{2,1,0:T(8,128)(2,1)S(1)} %copy-done.2, bf16[18,8,256]{2,1,0:T(8,128)(2,1)S(1)} %copy-done.4, bf16[256,512]{1,0:T(8,128)(2,1)S(1)} %copy-done, bf16[256,512]{1,0:T(8,128)(2,1)S(1)} %copy-done.1, bf16[48,512]{1,0:T(8,128)(2,1)S(1)} %bitcast.2, ...), custom_call_target="tpu_custom_call" | custom-call | tf_op jit(solution)/shard_map/pair_block/pallas_call | solution.py:334
Async XLA Ops:
  13.9 1.0 %copy-start = (bf16[256,512]{1,0:T(8,128)(2,1)S(1)}, bf16[256,512]{1,0:T(8,128)(2,1)}, u32[]{:S(2)}) copy-start(bf16[256,512]{1,0:T(8,128)(2,1)} %row_w_hbm.1) | copy-start | bytes 786436
  14.8 0.9 %copy-start.1 = (bf16[256,512]{1,0:T(8,128)(2,1)S(1)}, bf16[256,512]{1,0:T(8,128)(2,1)}, u32[]{:S(2)}) copy-start(bf16[256,512]{1,0:T(8,128)(2,1)} %col_w_hbm.1) | copy-start | bytes 786436
  15.8 0.9 %copy-start.2 = (bf16[34,8,256]{2,1,0:T(8,128)(2,1)S(1)}, bf16[34,8,256]{2,1,0:T(8,128)(2,1)}, u32[]{:S(2)}) copy-start(bf16[34,8,256]{2,1,0:T(8,128)(2,1)} %get-tuple-element.7.rows_hbm) | copy-start | bytes 417796
  16.7 0.9 %copy-start.3 = (bf16[3,3,48,48]{3,2,1,0:T(8,128)(2,1)S(1)}, bf16[3,3,48,48]{3,2,1,0:T(8,128)(2,1)}, u32[]{:S(2)}) copy-start(bf16[3,3,48,48]{3,2,1,0:T(8,128)(2,1)} %taps_hbm.1) | copy-start | bytes 124420
  17.6 0.9 %copy-start.4 = (bf16[18,8,256]{2,1,0:T(8,128)(2,1)S(1)}, bf16[18,8,256]{2,1,0:T(8,128)(2,1)}, u32[]{:S(2)}) copy-start(bf16[18,8,256]{2,1,0:T(8,128)(2,1)} %get-tuple-element.8.cols_hbm) | copy-start | bytes 221188
  18.5 0.8 %copy-start.5 = (bf16[512,48]{0,1:T(8,128)(2,1)S(1)}, bf16[512,48]{0,1:T(8,128)(2,1)}, u32[]{:S(2)}) copy-start(bf16[512,48]{0,1:T(8,128)(2,1)} %param.9) | copy-start | bytes 147460
  19.3 0.7 %copy-start.6 = (bf16[48,48]{1,0:T(8,128)(2,1)S(1)}, bf16[48,48]{1,0:T(8,128)(2,1)}, u32[]{:S(2)}) copy-start(bf16[48,48]{1,0:T(8,128)(2,1)} %mix_hbm.1) | copy-start | bytes 13828

commit v3 on v2

--- a/solution.py
+++ b/solution.py
@@ -286,23 +286,16 @@
 
     def conv_rows(m, carry):
         slot = lax.rem(m, 2)
+        mids = []
         for u in range(2):
-            p = 2 * m + u
-            at = pl.ds(pl.multiple_of(48 * p, 16), 144)
-            parts = [dot(tap_w, act[at, 256 * n : 256 * n + 256]) for n in range(9)]
-
-            def part(b, q):
-                return parts[q // 2][48 * b : 48 * b + 48, 128 * (q % 2) : 128 * (q % 2) + 128]
-
-            tiles = []
-            for n in range(8):
-                mids = [
-                    jnp.maximum(part(0, q - 1) + part(1, q) + part(2, q + 1), 0.0).astype(bf16)
-                    for q in (2 * n + 1, 2 * n + 2)
-                ]
-                here = base[pl.ds(pl.multiple_of(48 * (p + 1), 16), 48), 256 * n + 128 : 256 * n + 384]
-                cells = (dot(mix, jnp.concatenate(mids, axis=1)) + here.astype(f32)).astype(bf16)
-                tiles += [cells[:, :128], cells[:, 128:]]
+            at = pl.ds(pl.multiple_of(96 * m + 48 * u, 16), 144)
+            sums = dot(tap_w, act[at, :])
+            mids.append(jnp.maximum(sums[:48, :2048] + sums[48:96, 128:2176] + sums[96:, 256:], 0.0).astype(bf16))
+        mixed = [dot(mix, mids[u]) for u in range(2)]
+        for u in range(2):
+            here = base[pl.ds(pl.multiple_of(96 * m + 48 * u + 48, 16), 48), 128:2176]
+            cells = (mixed[u] + here.astype(f32)).astype(bf16)
+            tiles = [cells[:, 128 * q : 128 * q + 128] for q in range(16)]
             for d in (1, 2, 4, 8):
                 stay = (group & d) == 0
                 for q in range(16):
@@ -354,7 +347,7 @@
             pltpu.SemaphoreType.DMA((7,)),
             pltpu.SemaphoreType.DMA((2, 2)),
         ],
-        compiler_params=pltpu.CompilerParams(vmem_limit_bytes=48 << 20),
+        compiler_params=pltpu.CompilerParams(vmem_limit_bytes=(64 << 20) - (1 << 16)),
         name="pair_block",
     )(rows, cols, row_weight, column_weight, pair_map_weight.T, dilated_weight, mixing_weight)
 

time: 46.5 us -> 40.2 us (0.86)
  local copies, waits for them, and re-layouts: 6.09 us -> 0 us
    unnamed x14 -> x0, local copies, waits for them, and re-layouts: 6.09 us -> none
where the time goes in v3:
time: 40.2 us; the launch traced here: 40.1 us
  Pallas kernels  40.1 us (100%)
    pallas_call x1, Pallas kernels, block(): pl.pallas_call(block_kernel, out_shape=jax.ShapeDtypeStruct((48, 256, 128...  26.2 us
    pallas_call x1, Pallas kernels, gather(): pl.pallas_call(gather_kernel, out_shape=(jax.ShapeDtypeStruct((34, 8, wid...  13.8 us

profile of v3, /device:TPU:1, one launch (start us, length us, event | category | flops | bytes accessed | tf_op | source)
XLA Modules:
  0.0 40.1 jit_solution(3171310141999033911)
XLA Ops:
  0.0 13.8 %gather_bins.1 = (bf16[34,8,256]{2,1,0:T(8,128)(2,1)}, bf16[18,8,256]{2,1,0:T(8,128)(2,1)}) custom-call(bf16[2,8,256]{2,1,0:T(8,128)(2,1)} %bitcast.3), custom_call_target="tpu_custom_call" | custom-call | tf_op jit(solution)/shard_map/gather_bins/pallas_call | solution.py:181
  13.9 26.2 %pair_block.1 = bf16[48,256,128]{2,1,0:T(8,128)(2,1)} custom-call(bf16[34,8,256]{2,1,0:T(8,128)(2,1)} %get-tuple-element.7.rows_hbm, bf16[18,8,256]{2,1,0:T(8,128)(2,1)} %get-tuple-element.8.cols_hbm, bf16[256,512]{1,0:T(8,128)(2,1)} %row_w_hbm.1, bf16[256,512]{1,0:T(8,128)(2,1)} %col_w_hbm.1, bf16[48,512]{1,0:T(8,128)(2,1)} %bitcast.2, ...), custom_call_target="tpu_custom_call" | custom-call | tf_op jit(solution)/shard_map/pair_block/pallas_call | solution.py:327

commit v4 on v3

--- a/solution.py
+++ b/solution.py
@@ -204,7 +204,7 @@
 def block_kernel(
     rows_hbm, cols_hbm, row_w_hbm, col_w_hbm, pair_w_hbm, taps_hbm, mix_hbm, out_hbm,
     rows_in, cols_in, row_w_in, col_w_in, pair_w_in, taps_in, mix_in,
-    row_pat, col_pat, act, base, taps, turn, out_tile, in_sem, out_sem,
+    row_pat, col_pat, act, base, taps, turn, held, out_tile, in_sem, out_sem,
 ):
     r = lax.axis_index("row")
     c = lax.axis_index("col")
@@ -273,7 +273,7 @@
             base[at, 256 * n : 256 * n + 256] = hidden.astype(bf16)
         return carry
 
-    lax.fori_loop(0, 18, pair_rows, 0)
+    lax.fori_loop(0, 18, pair_rows, 0, unroll=6)
 
     mix = mix_in[...]
     tap_w = taps[...]
@@ -284,8 +284,7 @@
             out_tile.at[slot, e], out_hbm.at[:, pl.ds(pl.multiple_of(128 * e + 16 * m, 16), 16), :], out_sem.at[slot, e]
         )
 
-    def conv_rows(m, carry):
-        slot = lax.rem(m, 2)
+    def conv_rows(m):
         mids = []
         for u in range(2):
             at = pl.ds(pl.multiple_of(96 * m + 48 * u, 16), 144)
@@ -294,17 +293,22 @@
         mixed = [dot(mix, mids[u]) for u in range(2)]
         for u in range(2):
             here = base[pl.ds(pl.multiple_of(96 * m + 48 * u + 48, 16), 48), 128:2176]
-            cells = (mixed[u] + here.astype(f32)).astype(bf16)
-            tiles = [cells[:, 128 * q : 128 * q + 128] for q in range(16)]
+            held[u] = (mixed[u] + here.astype(f32)).astype(bf16)
+
+    def turn_rows(m):
+        for u in range(2):
+            tiles = [held[u, :, 128 * q : 128 * q + 128] for q in range(16)]
+            tiles = [pltpu.roll(tile, 8 * q, 1) if q else tile for q, tile in enumerate(tiles)]
+            tiles = [tiles[-k % 16] for k in range(16)]
             for d in (1, 2, 4, 8):
-                stay = (group & d) == 0
-                for q in range(16):
-                    if q & d == 0:
-                        x, y = tiles[q], tiles[q + d]
-                        tiles[q] = jnp.where(stay, x, pltpu.roll(y, 8 * d, 1))
-                        tiles[q + d] = jnp.where(stay, pltpu.roll(x, 128 - 8 * d, 1), y)
+                move = (group & d) != 0
+                tiles = [jnp.where(move, tiles[(k - d) % 16], tiles[k]) for k in range(16)]
+            tiles = [pltpu.roll(tile, 128 - 8 * k, 1) if k else tile for k, tile in enumerate(tiles)]
             for k in range(16):
-                turn[k // 8, pl.ds(8 * u + k % 8, 48, stride=16), :] = tiles[k].astype(f32)
+                turn[k // 8, u, pl.ds(k % 8, 48, stride=9), :] = tiles[k].astype(f32)
+
+    def put_rows(m):
+        slot = lax.rem(m, 2)
 
         @pl.when(m >= 2)
         def _():
@@ -312,11 +316,20 @@
                 store(slot, e, m - 2).wait()
 
         for e in range(2):
-            out_tile[slot, e] = turn[e].reshape(48, 16, 128).astype(bf16)
+            halves = [jnp.stack([turn[e, u, 9 * o : 9 * o + 8] for o in range(48)]) for u in range(2)]
+            out_tile[slot, e] = jnp.concatenate(halves, axis=1).astype(bf16)
             store(slot, e, m).start()
+
+    def step(m, carry):
+        turn_rows(m - 1)
+        conv_rows(m)
+        put_rows(m - 1)
         return carry
 
-    lax.fori_loop(0, 8, conv_rows, 0)
+    conv_rows(0)
+    lax.fori_loop(1, 8, step, 0)
+    turn_rows(7)
+    put_rows(jnp.int32(7))
     for m in (6, 7):
         for e in range(2):
             store(m % 2, e, m).wait()
@@ -342,7 +355,8 @@
             pltpu.VMEM((18 * 48, 18 * 128), bf16),
             pltpu.VMEM((18 * 48, 18 * 128), bf16),
             pltpu.VMEM((144, 144), bf16),
-            pltpu.VMEM((2, 768, 128), f32),
+            pltpu.VMEM((2, 2, 432, 128), f32),
+            pltpu.VMEM((2, 48, 2048), bf16),
             pltpu.VMEM((2, 2, 48, 16, 128), bf16),
             pltpu.SemaphoreType.DMA((7,)),
             pltpu.SemaphoreType.DMA((2, 2)),

time: 40.2 us -> 34.3 us (0.85)
  Pallas kernels: 40.1 us -> 34.1 us
    pallas_call x1, Pallas kernels: 26.2 us -> 20.3 us  [block(): pl.pallas_call(block_kernel, out_shape=jax.ShapeDtypeStruct((48, 256, 128...]
where the time goes in v4:
time: 34.3 us; the launch traced here: 34.1 us
  Pallas kernels  34.1 us (99%)
    pallas_call x1, Pallas kernels, block(): pl.pallas_call(block_kernel, out_shape=jax.ShapeDtypeStruct((48, 256, 128...  20.3 us
    pallas_call x1, Pallas kernels, gather(): pl.pallas_call(gather_kernel, out_shape=(jax.ShapeDtypeStruct((34, 8, wid...  13.8 us

profile of v4, /device:TPU:1, one launch (start us, length us, event | category | flops | bytes accessed | tf_op | source)
XLA Modules:
  0.0 34.1 jit_solution(8855186770402008552)
XLA Ops:
  0.0 13.8 %gather_bins.1 = (bf16[34,8,256]{2,1,0:T(8,128)(2,1)}, bf16[18,8,256]{2,1,0:T(8,128)(2,1)}) custom-call(bf16[2,8,256]{2,1,0:T(8,128)(2,1)} %bitcast.3), custom_call_target="tpu_custom_call" | custom-call | tf_op jit(solution)/shard_map/gather_bins/pallas_call | solution.py:181
  13.9 20.3 %pair_block.1 = bf16[48,256,128]{2,1,0:T(8,128)(2,1)} custom-call(bf16[34,8,256]{2,1,0:T(8,128)(2,1)} %get-tuple-element.7.rows_hbm, bf16[18,8,256]{2,1,0:T(8,128)(2,1)} %get-tuple-element.8.cols_hbm, bf16[256,512]{1,0:T(8,128)(2,1)} %row_w_hbm.1, bf16[256,512]{1,0:T(8,128)(2,1)} %col_w_hbm.1, bf16[48,512]{1,0:T(8,128)(2,1)} %bitcast.2, ...), custom_call_target="tpu_custom_call" | custom-call | tf_op jit(solution)/shard_map/pair_block/pallas_call | solution.py:340

commit v5 on v4

--- a/solution.py
+++ b/solution.py
@@ -185,7 +185,7 @@
             jax.ShapeDtypeStruct((18, 8, width), bf16),
         ),
         in_specs=[VMEM],
-        out_specs=(VMEM, VMEM),
+        out_specs=(pl.BlockSpec(memory_space=pltpu.HBM),) * 2,
         scratch_shapes=[
             pltpu.VMEM((8, width), bf16),
             pltpu.SemaphoreType.DMA,
@@ -273,7 +273,7 @@
             base[at, 256 * n : 256 * n + 256] = hidden.astype(bf16)
         return carry
 
-    lax.fori_loop(0, 18, pair_rows, 0, unroll=6)
+    lax.fori_loop(0, 18, pair_rows, 0, unroll=18)
 
     mix = mix_in[...]
     tap_w = taps[...]

time: 34.3 us -> 32.8 us (0.956)
  Pallas kernels: 34.1 us -> 32.6 us
    pallas_call x1, Pallas kernels: 20.3 us -> 19.3 us  [block(): pl.pallas_call(block_kernel, out_shape=jax.ShapeDtypeStruct((48, 256, 128...]
    pallas_call x1, Pallas kernels: 13.8 us -> 13.3 us  [gather(): pl.pallas_call(gather_kernel, out_shape=(jax.ShapeDtypeStruct((34, 8, wid...]
where the time goes in v5:
time: 32.8 us; the launch traced here: 32.6 us
  Pallas kernels  32.6 us (99%)
    pallas_call x1, Pallas kernels, block(): pl.pallas_call(block_kernel, out_shape=jax.ShapeDtypeStruct((48, 256, 128...  19.3 us
    pallas_call x1, Pallas kernels, gather(): pl.pallas_call(gather_kernel, out_shape=(jax.ShapeDtypeStruct((34, 8, wid...  13.3 us

profile of v5, /device:TPU:1, one launch (start us, length us, event | category | flops | bytes accessed | tf_op | source)
XLA Modules:
  0.0 32.6 jit_solution(8856359801242373846)
XLA Ops:
  0.0 13.3 %gather_bins.1 = (bf16[34,8,256]{2,1,0:T(8,128)(2,1)}, bf16[18,8,256]{2,1,0:T(8,128)(2,1)}) custom-call(bf16[2,8,256]{2,1,0:T(8,128)(2,1)} %bitcast.3), custom_call_target="tpu_custom_call" | custom-call | tf_op jit(solution)/shard_map/gather_bins/pallas_call | solution.py:181
  13.3 19.3 %pair_block.1 = bf16[48,256,128]{2,1,0:T(8,128)(2,1)} custom-call(bf16[34,8,256]{2,1,0:T(8,128)(2,1)} %get-tuple-element.7.rows_hbm, bf16[18,8,256]{2,1,0:T(8,128)(2,1)} %get-tuple-element.8.cols_hbm, bf16[256,512]{1,0:T(8,128)(2,1)} %row_w_hbm.1, bf16[256,512]{1,0:T(8,128)(2,1)} %col_w_hbm.1, bf16[48,512]{1,0:T(8,128)(2,1)} %bitcast.2, ...), custom_call_target="tpu_custom_call" | custom-call | tf_op jit(solution)/shard_map/pair_block/pallas_call | solution.py:340

commit v6 on v5

--- a/solution.py
+++ b/solution.py
@@ -230,13 +230,14 @@
     loads[1].wait()
     for n in range(9):
         cells = []
-        for p in (2 * n, 2 * n + 1):
+        for p in (2 * n, 2 * n + 1)[: 1 if n == 8 else 2]:
             for e in range(2):
-                bins = rows_in[16 * e + p].astype(f32)
+                bins = rows_in[33 * e if p == 16 else 16 * e + p + 1].astype(f32)
                 cells.append(jnp.broadcast_to(bins[:, None, :], (8, 8, 256)).reshape(64, 256))
         proj = dot(row_w, jnp.concatenate(cells, 0).astype(bf16), ((1,), (1,))).astype(bf16)
         row_pat[2 * n] = proj[:, :128]
-        row_pat[2 * n + 1] = proj[:, 128:]
+        if n < 8:
+            row_pat[2 * n + 1] = proj[:, 128:]
     loads[2].wait()
     col_w = col_w_in[...].T
     loads[3].wait()
@@ -256,24 +257,43 @@
     zero = jnp.zeros((), bf16)
     pair_w = pair_w_in[...]
 
+    not_first = (c > 0).astype(f32)
+    not_last = (c < 15).astype(f32)
+    left = lane < 64
+
+    def pair_chunk(row, n):
+        pair_act = jnp.concatenate(
+            [jnp.maximum(row + col_pat[2 * n], zero), jnp.maximum(row + col_pat[2 * n + 1], zero)], axis=1
+        )
+        hidden = dot(pair_w, pair_act)
+        shown = jnp.maximum(hidden, 0.0)
+        if n == 0:
+            shown = jnp.concatenate([shown[:, :128] * not_first, shown[:, 128:]], axis=1)
+        if n == 8:
+            shown = jnp.concatenate([shown[:, :128], shown[:, 128:] * not_last], axis=1)
+        return hidden, shown
+
     def pair_rows(p, carry):
         row = row_pat[p]
-        tile_row = 32 * r + 16 * (lane // 64) + p - 1
-        inside = ((tile_row >= 0) & (tile_row < 256)).astype(f32)
-        first = inside * (c > 0).astype(f32)
-        last = inside * (c < 15).astype(f32)
-        at = pl.ds(pl.multiple_of(48 * p, 16), 48)
+        at = pl.ds(pl.multiple_of(48 * p + 48, 16), 48)
         for n in range(9):
-            pair_act = jnp.concatenate(
-                [jnp.maximum(row + col_pat[2 * n], zero), jnp.maximum(row + col_pat[2 * n + 1], zero)], axis=1
-            )
-            hidden = dot(pair_w, pair_act)
-            keep = jnp.concatenate([first if n == 0 else inside, last if n == 8 else inside], axis=1)
-            act[at, 256 * n : 256 * n + 256] = (jnp.maximum(hidden, 0.0) * keep).astype(bf16)
+            hidden, shown = pair_chunk(row, n)
+            act[at, 256 * n : 256 * n + 256] = shown.astype(bf16)
             base[at, 256 * n : 256 * n + 256] = hidden.astype(bf16)
         return carry
 
-    lax.fori_loop(0, 18, pair_rows, 0, unroll=18)
+    lax.fori_loop(0, 16, pair_rows, 0, unroll=16)
+
+    inside = jnp.where(left, (r > 0).astype(f32), (r < 7).astype(f32))
+    inside = jnp.concatenate([inside, inside], axis=1)
+    halo_row = row_pat[16]
+    for n in range(9):
+        halo = (pair_chunk(halo_row, n)[1] * inside).astype(bf16)
+        for u in range(2):
+            at = slice(256 * n + 128 * u, 256 * n + 128 * u + 128)
+            outer = halo[:, 128 * u : 128 * u + 128]
+            act[0:48, at] = jnp.where(left, outer, pltpu.roll(act[768:816, at], 64, 1))
+            act[816:864, at] = jnp.where(left, pltpu.roll(act[48:96, at], 64, 1), outer)
 
     mix = mix_in[...]
     tap_w = taps[...]
@@ -350,7 +370,7 @@
             pltpu.VMEM((48, 512), bf16),
             pltpu.VMEM((3, 3, 48, 48), bf16),
             pltpu.VMEM((48, 48), bf16),
-            pltpu.VMEM((18, 512, 128), bf16),
+            pltpu.VMEM((17, 512, 128), bf16),
             pltpu.VMEM((18, 512, 128), bf16),
             pltpu.VMEM((18 * 48, 18 * 128), bf16),
             pltpu.VMEM((18 * 48, 18 * 128), bf16),

time: 32.8 us -> 32.1 us (0.979)
  Pallas kernels: 32.6 us -> 31.9 us
    pallas_call x1, Pallas kernels: 19.3 us -> 18.6 us  [block(): pl.pallas_call(block_kernel, out_shape=jax.ShapeDtypeStruct((48, 256, 128...]
where the time goes in v6:
time: 32.1 us; the launch traced here: 31.9 us
  Pallas kernels  31.9 us (99%)
    pallas_call x1, Pallas kernels, block(): pl.pallas_call(block_kernel, out_shape=jax.ShapeDtypeStruct((48, 256, 128...  18.6 us
    pallas_call x1, Pallas kernels, gather(): pl.pallas_call(gather_kernel, out_shape=(jax.ShapeDtypeStruct((34, 8, wid...  13.3 us

profile of v6, /device:TPU:1, one launch (start us, length us, event | category | flops | bytes accessed | tf_op | source)
XLA Modules:
  0.0 31.9 jit_solution(4551822851831712504)
XLA Ops:
  0.0 13.3 %gather_bins.1 = (bf16[34,8,256]{2,1,0:T(8,128)(2,1)}, bf16[18,8,256]{2,1,0:T(8,128)(2,1)}) custom-call(bf16[2,8,256]{2,1,0:T(8,128)(2,1)} %bitcast.3), custom_call_target="tpu_custom_call" | custom-call | tf_op jit(solution)/shard_map/gather_bins/pallas_call | solution.py:181
  13.3 18.6 %pair_block.1 = bf16[48,256,128]{2,1,0:T(8,128)(2,1)} custom-call(bf16[34,8,256]{2,1,0:T(8,128)(2,1)} %get-tuple-element.7.rows_hbm, bf16[18,8,256]{2,1,0:T(8,128)(2,1)} %get-tuple-element.8.cols_hbm, bf16[256,512]{1,0:T(8,128)(2,1)} %row_w_hbm.1, bf16[256,512]{1,0:T(8,128)(2,1)} %col_w_hbm.1, bf16[48,512]{1,0:T(8,128)(2,1)} %bitcast.2, ...), custom_call_target="tpu_custom_call" | custom-call | tf_op jit(solution)/shard_map/pair_block/pallas_call | solution.py:360

commit v7 on v6

--- a/solution.py
+++ b/solution.py
@@ -27,9 +27,8 @@
             body(n)
             return carry
 
-        lax.fori_loop(0, count, step, 0)
-
-    each(15, lambda n: signal(r, lax.rem(c + 1 + n, 16)))
+        lax.fori_loop(0, count, step, 0, unroll=True)
+
 
     @pl.when(r > 0)
     def _():
@@ -63,6 +62,8 @@
         @pl.when((row != r) | (col != c))
         def _():
             signal(row, col)
+
+    each(15, lambda n: signal(r, lax.rem(c + 1 + n, 16)))
 
     low_halo_rows = (c == 15) & (r < 7)
     high_halo_rows = (c == 0) & (r > 0)
@@ -228,7 +229,7 @@
     loads[0].wait()
     row_w = row_w_in[...].T
     loads[1].wait()
-    for n in range(9):
+    def row_patterns(n):
         cells = []
         for p in (2 * n, 2 * n + 1)[: 1 if n == 8 else 2]:
             for e in range(2):
@@ -238,6 +239,8 @@
         row_pat[2 * n] = proj[:, :128]
         if n < 8:
             row_pat[2 * n + 1] = proj[:, 128:]
+
+    row_patterns(0)
     loads[2].wait()
     col_w = col_w_in[...].T
     loads[3].wait()
@@ -273,16 +276,18 @@
             shown = jnp.concatenate([shown[:, :128], shown[:, 128:] * not_last], axis=1)
         return hidden, shown
 
-    def pair_rows(p, carry):
+    def pair_rows(p):
         row = row_pat[p]
-        at = pl.ds(pl.multiple_of(48 * p + 48, 16), 48)
+        at = slice(48 * p + 48, 48 * p + 96)
         for n in range(9):
             hidden, shown = pair_chunk(row, n)
             act[at, 256 * n : 256 * n + 256] = shown.astype(bf16)
             base[at, 256 * n : 256 * n + 256] = hidden.astype(bf16)
-        return carry
-
-    lax.fori_loop(0, 16, pair_rows, 0, unroll=16)
+
+    for n in range(1, 9):
+        row_patterns(n)
+        pair_rows(2 * n - 2)
+        pair_rows(2 * n - 1)
 
     inside = jnp.where(left, (r > 0).astype(f32), (r < 7).astype(f32))
     inside = jnp.concatenate([inside, inside], axis=1)
@@ -327,29 +332,35 @@
             for k in range(16):
                 turn[k // 8, u, pl.ds(k % 8, 48, stride=9), :] = tiles[k].astype(f32)
 
+    def pack_rows(m):
+        for e in range(2):
+            halves = [jnp.stack([turn[e, u, 9 * o : 9 * o + 8] for o in range(48)]) for u in range(2)]
+            out_tile[lax.rem(m, 2), e] = jnp.concatenate(halves, axis=1).astype(bf16)
+
     def put_rows(m):
-        slot = lax.rem(m, 2)
-
-        @pl.when(m >= 2)
+        for e in range(2):
+            store(lax.rem(m, 2), e, m).start()
+
+    def step(m, carry):
+        @pl.when(m >= 3)
         def _():
             for e in range(2):
-                store(slot, e, m - 2).wait()
-
-        for e in range(2):
-            halves = [jnp.stack([turn[e, u, 9 * o : 9 * o + 8] for o in range(48)]) for u in range(2)]
-            out_tile[slot, e] = jnp.concatenate(halves, axis=1).astype(bf16)
-            store(slot, e, m).start()
-
-    def step(m, carry):
+                store(lax.rem(m - 1, 2), e, m - 3).wait()
+
         turn_rows(m - 1)
+        pack_rows(m - 1)
         conv_rows(m)
         put_rows(m - 1)
         return carry
 
     conv_rows(0)
     lax.fori_loop(1, 8, step, 0)
-    turn_rows(7)
-    put_rows(jnp.int32(7))
+    last = jnp.int32(7)
+    for e in range(2):
+        store(1, e, 5).wait()
+    turn_rows(last)
+    pack_rows(last)
+    put_rows(last)
     for m in (6, 7):
         for e in range(2):
             store(m % 2, e, m).wait()

time: 32.1 us -> 31.6 us (0.984)
  Pallas kernels: 31.9 us -> 31.4 us
where the time goes in v7:
time: 31.6 us; the launch traced here: 31.4 us
  Pallas kernels  31.4 us (99%)
    pallas_call x1, Pallas kernels, block(): pl.pallas_call(block_kernel, out_shape=jax.ShapeDtypeStruct((48, 256, 128...  18.3 us
    pallas_call x1, Pallas kernels, gather(): pl.pallas_call(gather_kernel, out_shape=(jax.ShapeDtypeStruct((34, 8, wid...  13.1 us

profile of v7, /device:TPU:1, one launch (start us, length us, event | category | flops | bytes accessed | tf_op | source)
XLA Modules:
  0.0 31.4 jit_solution(15355507886690664140)
XLA Ops:
  0.0 13.1 %gather_bins.1 = (bf16[34,8,256]{2,1,0:T(8,128)(2,1)}, bf16[18,8,256]{2,1,0:T(8,128)(2,1)}) custom-call(bf16[2,8,256]{2,1,0:T(8,128)(2,1)} %bitcast.3), custom_call_target="tpu_custom_call" | custom-call | tf_op jit(solution)/shard_map/gather_bins/pallas_call | solution.py:182
  13.2 18.3 %pair_block.1 = bf16[48,256,128]{2,1,0:T(8,128)(2,1)} custom-call(bf16[34,8,256]{2,1,0:T(8,128)(2,1)} %get-tuple-element.7.rows_hbm, bf16[18,8,256]{2,1,0:T(8,128)(2,1)} %get-tuple-element.8.cols_hbm, bf16[256,512]{1,0:T(8,128)(2,1)} %row_w_hbm.1, bf16[256,512]{1,0:T(8,128)(2,1)} %col_w_hbm.1, bf16[48,512]{1,0:T(8,128)(2,1)} %bitcast.2, ...), custom_call_target="tpu_custom_call" | custom-call | tf_op jit(solution)/shard_map/pair_block/pallas_call | solution.py:371
